TPU v7x, 32 devices: a whole 2x2x4 slice. The times are simulated.
32 devices in a mesh: dp: 8 (over y, x, core), seq: 4 (over z).
Axes of the slice: x: 2, y: 2, z: 4, core: 2. Of those that a mesh axis runs over, the one named last changes fastest.
Arguments:
- block_input: bfloat16 [8, 1024, 2048], P('dp', 'seq'), may hold values from -6 to 6
- norm_gain: float32 [2048], replicated, may hold values from 0.5 to 1.5
- in_proj: bfloat16 [2048, 2816], P(('dp', 'seq')), may hold values from -0.125 to 0.125
- gate_proj: bfloat16 [2048, 2816], P(('dp', 'seq')), may hold values from -0.125 to 0.125
- conv_kernel: float32 [4, 2816], replicated, may hold values from -3 to 3
- conv_bias: float32 [2816], replicated, may hold values from -3 to 3
- recur_weight: bfloat16 [16, 176, 176], replicated, may hold values from -0.4375 to 0.4375
- recur_bias: float32 [2816], replicated, may hold values from -3 to 3
- input_weight: bfloat16 [16, 176, 176], replicated, may hold values from -0.4375 to 0.4375
- input_bias: float32 [2816], replicated, may hold values from -3 to 3
- decay_param: float32 [2816], replicated, may hold values from 5 to 10
- out_proj: bfloat16 [2816, 2048], P(('dp', 'seq')), may hold values from -0.3125 to 0.3125
- mlp_gain: float32 [2048], replicated, may hold values from 0.5 to 1.5
- mlp_gate: bfloat16 [2048, 6144], P(('dp', 'seq')), may hold values from -0.125 to 0.125
- mlp_up: bfloat16 [2048, 6144], P(('dp', 'seq')), may hold values from -0.125 to 0.125
- mlp_down: bfloat16 [6144, 2048], P(('dp', 'seq')), may hold values from -0.109375 to 0.109375
- out_grad: bfloat16 [8, 1024, 2048], P('dp', 'seq'), may hold values from -6 to 6
Outputs:
- block_output: bfloat16 [8, 1024, 2048], P('dp', 'seq')
- input_grad: float32 [8, 1024, 2048], P('dp', 'seq')
- grad_norm_gain: float32 [2048], replicated
- grad_in_proj: float32 [2048, 2816], P('seq', 'dp')
- grad_gate_proj: float32 [2048, 2816], P('seq', 'dp')
- grad_conv_kernel: float32 [4, 2816], replicated
- grad_conv_bias: float32 [2816], replicated
- grad_recur_weight: float32 [16, 176, 176], replicated
- grad_recur_bias: float32 [2816], replicated
- grad_input_weight: float32 [16, 176, 176], replicated
- grad_input_bias: float32 [2816], replicated
- grad_decay_param: float32 [2816], replicated
- grad_out_proj: float32 [2816, 2048], P('seq', 'dp')
- grad_mlp_gain: float32 [2048], replicated
- grad_mlp_gate: float32 [2048, 6144], P('seq', 'dp')
- grad_mlp_up: float32 [2048, 6144], P('seq', 'dp')
- grad_mlp_down: float32 [6144, 2048], P('seq', 'dp')
All inputs are finite; a program needn't handle non-finite values.
Results may differ from a plain program's by a relative error of at most 0.015.
Values may be sent and summed in bfloat16 or wider, within the bound.
No kernel may reach another device: no remote copies, remote signals or barrier semaphores. Data moves between devices by JAX's collectives and lax.ppermute only.
A program may use at most 640 MiB of HBM per device.

v0:
```python
import jax
import jax.numpy as jnp
from jax import lax
from jax.sharding import PartitionSpec as P

EPSILON = 1e-06


def from_behind(value, axis, steps):
    count = lax.axis_size(axis)
    initial, last = (max(0, -steps), min(count, count - steps))
    return lax.ppermute(value, axis, [(source, source + steps) for source in range(initial, last)])


def scaled_norm(values, gain_vec):
    return (
        values * lax.rsqrt(jnp.mean(values * values, axis=-1, keepdims=True) + EPSILON) * gain_vec
    )


def recurrence_gates(recur_pre, input_pre, conv_out, decay_param):
    recur_gate = jax.nn.sigmoid(recur_pre)
    input_gate = jax.nn.sigmoid(input_pre)
    log_rate = -8.0 * recur_gate * jax.nn.softplus(-decay_param)
    decay_rate = jnp.exp(log_rate)
    driven = jnp.sqrt(-jnp.expm1(2.0 * log_rate)) * input_gate * conv_out
    return (decay_rate, driven)


def gated_product(gate_values, up_values):
    return jax.nn.gelu(gate_values) * up_values


def compose(earlier, later):
    return (earlier[0] * later[0], earlier[1] * later[0] + later[1])


def matmul_back(grad_rows, weight_full):
    return lax.dot_general(
        grad_rows, weight_full, (((1,), (1,)), ((), ())), preferred_element_type=jnp.float32
    )


def reduce_weight_grad(left_side, right_side):
    inner_sum = lax.psum_scatter(
        lax.dot_general(
            left_side, right_side, (((0,), (0,)), ((), ())), preferred_element_type=jnp.float32
        ).astype(jnp.bfloat16),
        "seq",
        scatter_dimension=0,
        tiled=True,
    )
    return lax.psum_scatter(inner_sum, "dp", scatter_dimension=1, tiled=True).astype(jnp.float32)


def local(
    block_input,
    norm_gain,
    in_proj,
    gate_proj,
    conv_kernel,
    conv_bias,
    recur_weight,
    recur_bias,
    input_weight,
    input_bias,
    decay_param,
    out_proj,
    mlp_gain,
    mlp_gate,
    mlp_up,
    mlp_down,
    out_grad,
):
    seq_count = lax.axis_size("seq")
    model_width = block_input.shape[2]
    tokens = block_input.reshape(-1, model_width).astype(jnp.float32)
    length = tokens.shape[0]
    head_count = recur_weight.shape[0]
    head_size = recur_weight.shape[1]
    tap_count = conv_kernel.shape[0]
    conv_lag = tap_count - 1
    fwd_recur = (
        lax.all_gather(in_proj, ("dp", "seq"), axis=0, tiled=True),
        lax.all_gather(gate_proj, ("dp", "seq"), axis=0, tiled=True),
        lax.all_gather(out_proj, ("dp", "seq"), axis=0, tiled=True),
    )
    normed = scaled_norm(tokens, norm_gain).astype(jnp.bfloat16)
    branch = jnp.dot(normed, fwd_recur[0], preferred_element_type=jnp.float32)
    gate_pre = jnp.dot(normed, fwd_recur[1], preferred_element_type=jnp.float32)
    gate_act = jax.nn.gelu(gate_pre)
    recur_width = branch.shape[1]
    prior_rows = from_behind(branch[length - conv_lag :], "seq", 1)
    padded = jnp.concatenate([prior_rows, branch], axis=0)
    conv_out = jnp.zeros((length, recur_width), jnp.float32) + conv_bias
    for tap_index in range(tap_count):
        begin = conv_lag - tap_index
        conv_out = conv_out + conv_kernel[tap_index] * padded[begin : begin + length]
    heads_in = conv_out.astype(jnp.bfloat16).reshape(length, head_count, head_size)
    recur_pre = (
        jnp.einsum(
            "thi,hij->thj", heads_in, recur_weight, preferred_element_type=jnp.float32
        ).reshape(length, recur_width)
        + recur_bias
    )
    input_pre = (
        jnp.einsum(
            "thi,hij->thj", heads_in, input_weight, preferred_element_type=jnp.float32
        ).reshape(length, recur_width)
        + input_bias
    )
    decay_rate, driven = recurrence_gates(recur_pre, input_pre, conv_out, decay_param)
    decay_run, local_states = lax.associative_scan(compose, (decay_rate, driven), axis=0)
    zero_row = jnp.zeros((recur_width,), jnp.float32)
    carried = zero_row
    for repeat in range(seq_count - 1):
        carried = from_behind(decay_run[length - 1] * carried + local_states[length - 1], "seq", 1)
    states = local_states + decay_run * carried
    mixed_out = (states * gate_act).astype(jnp.bfloat16)
    residual = tokens + jnp.dot(mixed_out, fwd_recur[2], preferred_element_type=jnp.float32)
    fwd_ffn = (
        lax.all_gather(mlp_gate, ("dp", "seq"), axis=0, tiled=True),
        lax.all_gather(mlp_up, ("dp", "seq"), axis=0, tiled=True),
        lax.all_gather(mlp_down, ("dp", "seq"), axis=0, tiled=True),
    )
    normed_two = scaled_norm(residual, mlp_gain).astype(jnp.bfloat16)
    ffn_gate = jnp.dot(normed_two, fwd_ffn[0], preferred_element_type=jnp.float32)
    ffn_up = jnp.dot(normed_two, fwd_ffn[1], preferred_element_type=jnp.float32)
    hidden = gated_product(ffn_gate, ffn_up).astype(jnp.bfloat16)
    result = residual + jnp.dot(hidden, fwd_ffn[2], preferred_element_type=jnp.float32)
    block_output = result.astype(jnp.bfloat16).reshape(block_input.shape)
    back_recur = (
        lax.all_gather(in_proj, ("dp", "seq"), axis=0, tiled=True),
        lax.all_gather(gate_proj, ("dp", "seq"), axis=0, tiled=True),
        lax.all_gather(out_proj, ("dp", "seq"), axis=0, tiled=True),
    )
    back_ffn = (
        lax.all_gather(mlp_gate, ("dp", "seq"), axis=0, tiled=True),
        lax.all_gather(mlp_up, ("dp", "seq"), axis=0, tiled=True),
        lax.all_gather(mlp_down, ("dp", "seq"), axis=0, tiled=True),
    )
    grad_low = out_grad.reshape(length, model_width)
    grad_top = grad_low.astype(jnp.float32)
    grad_down_w = reduce_weight_grad(hidden, grad_low)
    grad_hidden = matmul_back(grad_low, back_ffn[2])
    unused, pull_ffn = jax.vjp(gated_product, ffn_gate, ffn_up)
    grad_ffn_gate, grad_ffn_up = pull_ffn(grad_hidden)
    grad_ffn_gate = grad_ffn_gate.astype(jnp.bfloat16)
    grad_ffn_up = grad_ffn_up.astype(jnp.bfloat16)
    grad_mgate_w = reduce_weight_grad(normed_two, grad_ffn_gate)
    grad_mup_w = reduce_weight_grad(normed_two, grad_ffn_up)
    grad_normed_two = matmul_back(grad_ffn_gate, back_ffn[0]) + matmul_back(
        grad_ffn_up, back_ffn[1]
    )
    unused, pull_norm_two = jax.vjp(scaled_norm, residual, mlp_gain)
    grad_resid_part, mlp_gain_term = pull_norm_two(grad_normed_two)
    grad_residual = grad_resid_part + grad_top
    grad_rec = grad_residual.astype(jnp.bfloat16)
    grad_out_w = reduce_weight_grad(mixed_out, grad_rec)
    grad_mixed = matmul_back(grad_rec, back_recur[2])
    grad_states = grad_mixed * gate_act
    unused, pull_gelu = jax.vjp(jax.nn.gelu, gate_pre)
    grad_gate_pre = pull_gelu(grad_mixed * states)[0].astype(jnp.bfloat16)
    next_decay = jnp.concatenate([decay_rate[1:], jnp.ones((1, recur_width), jnp.float32)], axis=0)
    decay_tail, local_grads = lax.associative_scan(
        compose, (next_decay, grad_states), reverse=True, axis=0
    )
    total_decay = decay_rate[0] * decay_tail[0]
    first_grad = decay_rate[0] * local_grads[0]
    later_grad = zero_row
    for repeat in range(seq_count - 1):
        later_grad = from_behind(total_decay * later_grad + first_grad, "seq", -1)
    state_grads = local_grads + decay_tail * later_grad
    prior_states = jnp.concatenate([carried[None], states[: length - 1]], axis=0)
    unused, pull_gates = jax.vjp(recurrence_gates, recur_pre, input_pre, conv_out, decay_param)
    grad_recur_pre, grad_input_pre, grad_conv, decay_term = pull_gates(
        (state_grads * prior_states, state_grads)
    )
    grad_recur_low = grad_recur_pre.astype(jnp.bfloat16).reshape(length, head_count, head_size)
    grad_input_low = grad_input_pre.astype(jnp.bfloat16).reshape(length, head_count, head_size)
    recur_w_term = jnp.einsum(
        "thi,thj->hij", heads_in, grad_recur_low, preferred_element_type=jnp.float32
    )
    input_w_term = jnp.einsum(
        "thi,thj->hij", heads_in, grad_input_low, preferred_element_type=jnp.float32
    )
    recur_b_term = jnp.sum(grad_recur_low.astype(jnp.float32), axis=0).reshape(recur_width)
    input_b_term = jnp.sum(grad_input_low.astype(jnp.float32), axis=0).reshape(recur_width)
    grad_conv = grad_conv + jnp.einsum(
        "thj,hij->thi", grad_recur_low, recur_weight, preferred_element_type=jnp.float32
    ).reshape(length, recur_width)
    grad_conv = grad_conv + jnp.einsum(
        "thj,hij->thi", grad_input_low, input_weight, preferred_element_type=jnp.float32
    ).reshape(length, recur_width)
    later_rows = from_behind(grad_conv[:conv_lag].astype(jnp.bfloat16), "seq", -1).astype(
        jnp.float32
    )
    grad_padded = jnp.concatenate([grad_conv, later_rows], axis=0)
    grad_branch = jnp.zeros((length, recur_width), jnp.float32)
    kernel_rows = []
    for tap_index in range(tap_count):
        grad_branch = (
            grad_branch + conv_kernel[tap_index] * grad_padded[tap_index : tap_index + length]
        )
        begin = conv_lag - tap_index
        kernel_rows.append(jnp.sum(grad_conv * padded[begin : begin + length], axis=0))
    kernel_term = jnp.stack(kernel_rows, axis=0)
    bias_term = jnp.sum(grad_conv, axis=0)
    grad_branch = grad_branch.astype(jnp.bfloat16)
    grad_in_w = reduce_weight_grad(normed, grad_branch)
    grad_gate_w = reduce_weight_grad(normed, grad_gate_pre)
    grad_normed = matmul_back(grad_branch, back_recur[0]) + matmul_back(
        grad_gate_pre, back_recur[1]
    )
    unused, pull_norm = jax.vjp(scaled_norm, tokens, norm_gain)
    grad_tokens, norm_gain_term = pull_norm(grad_normed)
    input_grad = (grad_tokens + grad_residual).reshape(block_input.shape)
    summed = lax.psum(
        (
            norm_gain_term,
            kernel_term,
            bias_term,
            recur_w_term,
            recur_b_term,
            input_w_term,
            input_b_term,
            decay_term,
            mlp_gain_term,
        ),
        ("dp", "seq"),
    )
    return (
        block_output,
        input_grad,
        summed[0],
        grad_in_w,
        grad_gate_w,
        summed[1],
        summed[2],
        summed[3],
        summed[4],
        summed[5],
        summed[6],
        summed[7],
        grad_out_w,
        summed[8],
        grad_mgate_w,
        grad_mup_w,
        grad_down_w,
    )


def solution(mesh):
    return jax.shard_map(
        local,
        mesh=mesh,
        in_specs=(
            P("dp", "seq", None),
            P(),
            P(("dp", "seq"), None),
            P(("dp", "seq"), None),
            P(),
            P(),
            P(),
            P(),
            P(),
            P(),
            P(),
            P(("dp", "seq"), None),
            P(),
            P(("dp", "seq"), None),
            P(("dp", "seq"), None),
            P(("dp", "seq"), None),
            P("dp", "seq", None),
        ),
        out_specs=(
            P("dp", "seq", None),
            P("dp", "seq", None),
            P(),
            P("seq", "dp"),
            P("seq", "dp"),
            P(),
            P(),
            P(),
            P(),
            P(),
            P(),
            P(),
            P("seq", "dp"),
            P(),
            P("seq", "dp"),
            P("seq", "dp"),
            P("seq", "dp"),
        ),
        check_vma=False,
    )
```

profile of v0, /device:TPU:0, one launch (start us, length us, event | category | flops | bytes accessed | tf_op | source)
XLA Modules:
  0.0 3378.2 jit_solution(6021144712687071717)
XLA Ops:
  11.6 93.3 %all-gather.7.cloned.1.call-done = bf16[2048,2816]{1,0:T(8,128)(2,1)} async-done(((bf16[64,2816]{1,0:T(8,128)(2,1)}), bf16[2048,2816]{1,0:T(8,128)(2,1)}) %all-gather.7.cloned.1.call-update) | async-done | bytes 11534352 | tf_op jit(solution)/shard_map/all_gather | solution.py:84
  136.8 9.1 multiply_exponential_fusion
  324.3 9.6 pad.228
  333.9 9.4 pad.229
  345.9 9.4 pad.212
  355.3 9.3 pad.213
  384.0 13.3 multiply_convert_fusion.2
  405.5 40.2 %all-gather.13.cloned.1.call-done = bf16[2048,6144]{1,0:T(8,128)(2,1)} async-done(((bf16[64,6144]{1,0:T(8,128)(2,1)}), bf16[2048,6144]{1,0:T(8,128)(2,1)}) %all-gather.13.cloned.1.call-update) | async-done | bytes 25165840 | tf_op jit(solution)/shard_map/all_gather | solution.py:122
  445.7 14.2 fusion.108
  460.0 141.4 %all-gather.15.cloned.1.call-done = bf16[2048,6144]{1,0:T(8,128)(2,1)} async-done(((bf16[64,6144]{1,0:T(8,128)(2,1)}), bf16[2048,6144]{1,0:T(8,128)(2,1)}) %all-gather.15.cloned.1.call-update) | async-done | bytes 25165840 | tf_op jit(solution)/shard_map/all_gather | solution.py:123
  601.3 14.4 fusion.109
  615.7 141.2 %all-gather.17.cloned.1.call-done = bf16[6144,2048]{1,0:T(8,128)(2,1)} async-done(((bf16[192,2048]{1,0:T(8,128)(2,1)}), bf16[6144,2048]{1,0:T(8,128)(2,1)}) %all-gather.17.cloned.1.call-update) | async-done | bytes 25165840 | tf_op jit(solution)/shard_map/all_gather | solution.py:124
  756.9 22.1 multiply_convert_fusion
  779.0 13.5 fusion.110
  792.6 15.7 multiply_reduce_fusion.5
  811.6 12.8 fusion.45
  852.9 11.9 slice.637
  864.7 11.9 slice.643
  876.6 12.0 slice.695
  899.9 11.9 slice.634
  911.8 11.9 slice.639
  950.3 9.5 convolution_convert_fusion.5
  1068.7 9.5 pad.261
  1091.5 9.4 pad.245
  1100.9 12.0 slice.697
  1119.5 9.4 pad.244
  1131.4 9.6 pad.260
  1168.2 23.0 rev.9
  1191.1 22.7 rev.8
  1213.9 8.5 multiply_reduce_fusion
  1248.1 12.1 multiply_reduce_fusion.3
  1276.9 13.7 convolution_convert_fusion.2
  1290.7 13.8 convolution_convert_fusion.1
  1305.8 14.0 convolution_convert_fusion
  1325.1 144.4 %reduce-scatter.17.cloned.1.call-done = bf16[512,2816]{1,0:T(8,128)(2,1)} async-done(((bf16[2048,2816]{1,0:T(8,128)(2,1)}), bf16[512,2816]{1,0:T(8,128)(2,1)}) %reduce-scatter.17.cloned.1.call-update) | async-done | bytes 2883600 | tf_op jit(solution)/shard_map/reduce_scatter | solution.py:45
  1474.1 413.1 %reduce-scatter.25.cloned.1.call-done = bf16[512,6144]{1,0:T(8,128)(2,1)} async-done(((bf16[2048,6144]{1,0:T(8,128)(2,1)}), bf16[512,6144]{1,0:T(8,128)(2,1)}) %reduce-scatter.25.cloned.1.call-update) | async-done | bytes 6291472 | tf_op jit(solution)/shard_map/reduce_scatter | solution.py:45
  1887.2 418.7 %reduce-scatter.29.cloned.1.call-done = bf16[512,6144]{1,0:T(8,128)(2,1)} async-done(((bf16[2048,6144]{1,0:T(8,128)(2,1)}), bf16[512,6144]{1,0:T(8,128)(2,1)}) %reduce-scatter.29.cloned.1.call-update) | async-done | bytes 6291472 | tf_op jit(solution)/shard_map/reduce_scatter | solution.py:45
  2306.0 418.4 %reduce-scatter.33.cloned.1.call-done = bf16[1536,2048]{1,0:T(8,128)(2,1)} async-done(((bf16[6144,2048]{1,0:T(8,128)(2,1)}), bf16[1536,2048]{1,0:T(8,128)(2,1)}) %reduce-scatter.33.cloned.1.call-update) | async-done | bytes 6291472 | tf_op jit(solution)/shard_map/reduce_scatter | solution.py:45
  2734.0 10.0 fusion.37
  2748.2 14.7 fusion.35
  2764.8 10.6 reduce-scatter.39.cloned.1.call-done
  2777.7 45.9 %reduce-scatter.23.cloned.1.call-done = bf16[704,256]{1,0:T(8,128)(2,1)} async-done(((bf16[704,2048]{1,0:T(8,128)(2,1)}), bf16[704,256]{1,0:T(8,128)(2,1)}) %reduce-scatter.23.cloned.1.call-update) | async-done | bytes 360464 | tf_op jit(solution)/shard_map/reduce_scatter | solution.py:53
  2825.5 47.2 %reduce-scatter.37.cloned.1.call-done = bf16[352,512]{1,0:T(8,128)(2,1)} async-done(((bf16[2816,512]{1,0:T(8,128)(2,1)}), bf16[352,512]{1,0:T(8,128)(2,1)}) %reduce-scatter.37.cloned.1.call-update) | async-done | bytes 360464
  2875.0 62.7 %reduce-scatter.27.cloned.1.call-done = bf16[512,768]{1,0:T(8,128)(2,1)} async-done(((bf16[512,6144]{1,0:T(8,128)(2,1)}), bf16[512,768]{1,0:T(8,128)(2,1)}) %reduce-scatter.27.cloned.1.call-update) | async-done | bytes 786448 | tf_op jit(solution)/shard_map/reduce_scatter | solution.py:53
  2940.1 63.0 %reduce-scatter.31.cloned.1.call-done = bf16[512,768]{1,0:T(8,128)(2,1)} async-done(((bf16[512,6144]{1,0:T(8,128)(2,1)}), bf16[512,768]{1,0:T(8,128)(2,1)}) %reduce-scatter.31.cloned.1.call-update) | async-done | bytes 786448 | tf_op jit(solution)/shard_map/reduce_scatter | solution.py:53
  3005.5 62.6 %reduce-scatter.35.cloned.1.call-done = bf16[1536,256]{1,0:T(8,128)(2,1)} async-done(((bf16[1536,2048]{1,0:T(8,128)(2,1)}), bf16[1536,256]{1,0:T(8,128)(2,1)}) %reduce-scatter.35.cloned.1.call-update) | async-done | bytes 786448 | tf_op jit(solution)/shard_map/reduce_scatter | solution.py:53
  3070.5 130.0 %all-reduce.71.cloned.1.call-done = (f32[2048]{0:T(1024)}, f32[4,2816]{1,0:T(4,128)}, f32[2816]{0:T(1024)}, f32[2816]{0:T(1024)}, f32[2816]{0:T(1024)}, /*index=5*/f32[2816]{0:T(1024)}, f32[2048]{0:T(1024)}) async-done(((f32[2048]{0:T(1024)}, f32[4,2816]{1,0:T(4,128)}, f32[2816]{0:T(1024)}, f32[2816]{0:T(1024)}, f32[2816]{0:T(1024)}, /*index=5*/f32[2816]{0:T(1024)}, f32[2048]{0:T(1024)}), (f32[2048]{0:T(1024)}, ...) | async-done | bytes 106512 | tf_op jit(solution)/shard_map/psum | solution.py:218
  3200.5 158.8 %all-reduce.73.cloned.1.call-done = (f32[16,176,176]{2,1,0:T(8,128)}, f32[16,176,176]{2,1,0:T(8,128)}) async-done(((f32[16,176,176]{2,1,0:T(8,128)}, f32[16,176,176]{2,1,0:T(8,128)}), (f32[16,176,176]{2,1,0:T(8,128)}, f32[16,176,176]{2,1,0:T(8,128)})) %all-reduce.73.cloned.1.call-update) | async-done | bytes 3964944 | tf_op jit(solution)/shard_map/psum | solution.py:218
  (602 shorter events, 566.1 us)
Async XLA Ops:
  7.2 115.0 %copy-start = (bf16[16,176,176]{2,1,0:T(8,128)(2,1)S(1)}, bf16[16,176,176]{2,1,0:T(8,128)(2,1)}, u32[]{:S(2)}) copy-start(bf16[16,176,176]{2,1,0:T(8,128)(2,1)} %param.23) | copy-start | bytes 2973700
  7.2 97.7 %copy-start.41 = (f32[2048]{0:T(1024)S(1)}, f32[2048]{0:T(1024)}, u32[]{:S(2)}) copy-start(f32[2048]{0:T(1024)} %param.18) | copy-start | bytes 24580
  7.2 97.7 %all-gather.7.cloned.1.call-start = ((), (), s32[]{:S(2)}) async-start(), calls=%async_computation.12 | async-start | bytes 11894784 | tf_op jit(solution)/shard_map/all_gather | solution.py:84
  8.0 374.6 %all-gather.9.cloned.1.call-start = ((), (), s32[]{:S(2)}) async-start(), calls=%async_computation.13 | async-start | bytes 11894784 | tf_op jit(solution)/shard_map/all_gather | solution.py:85
  8.7 388.6 %all-gather.11.cloned.1.call-start = ((), (), s32[]{:S(2)}) async-start(), calls=%async_computation.14 | async-start | bytes 11894784 | tf_op jit(solution)/shard_map/all_gather | solution.py:86
  9.5 436.3 %all-gather.13.cloned.1.call-start = ((), (), s32[]{:S(2)}) async-start(), calls=%async_computation.15 | async-start | bytes 25952256 | tf_op jit(solution)/shard_map/all_gather | solution.py:122
  10.0 591.3 %all-gather.15.cloned.1.call-start = ((), (), s32[]{:S(2)}) async-start(), calls=%async_computation.16 | async-start | bytes 25952256 | tf_op jit(solution)/shard_map/all_gather | solution.py:123
  10.6 746.3 %all-gather.17.cloned.1.call-start = ((), (), s32[]{:S(2)}) async-start(), calls=%async_computation.17 | async-start | bytes 25952256 | tf_op jit(solution)/shard_map/all_gather | solution.py:124
  11.2 1308.7 %reduce-scatter.19.cloned.1.call-start = ((), (), s32[]{:S(2)}) async-start(), calls=%async_computation.19 | async-start | bytes 14417920 | tf_op jit(solution)/shard_map/reduce_scatter | solution.py:45
  11.5 99.7 %copy-start.112 = (f32[256]{0:T(256)}, f32[256]{0:T(256)S(1)}, u32[]{:S(2)}) copy-start(f32[256]{0:T(256)S(1)} %fusion.41) | copy-start | bytes 3076
  11.6 125.2 %copy-start.44 = (f32[2816]{0:T(1024)}, f32[2816]{0:T(1024)S(1)}, u32[]{:S(2)}) copy-start(f32[2816]{0:T(1024)S(1)} %broadcast_multiply_fusion) | copy-start | bytes 33796
  11.6 102.9 %copy-start.97 = (f32[4,2816]{1,0:T(4,128)S(1)}, f32[4,2816]{1,0:T(4,128)}, u32[]{:S(2)}) copy-start(f32[4,2816]{1,0:T(4,128)} %param.21) | copy-start | bytes 135172
  11.6 105.1 %copy-start.108 = (f32[2816]{0:T(1024)S(1)}, f32[2816]{0:T(1024)}, u32[]{:S(2)}) copy-start(f32[2816]{0:T(1024)} %param.22) | copy-start | bytes 33796
  111.3 5.5 collective-permute-start
  366.6 5.7 collective-permute-start.1
  372.3 5.8 collective-permute-start.2
  378.2 5.8 collective-permute-start.3
  405.5 195.8 %copy-start.14 = (bf16[256,2048]{1,0:T(8,128)(2,1)}, bf16[256,2048]{1,0:T(8,128)(2,1)S(1)}, u32[]{:S(2)}) copy-start(bf16[256,2048]{1,0:T(8,128)(2,1)S(1)} %multiply_convert_fusion.3) | copy-start | bytes 3145732
  831.9 492.6 %reduce-scatter.21.cloned.1.call-start = ((), (), s32[]{:S(2)}) async-start(), calls=%async_computation.20 | async-start | bytes 14417920 | tf_op jit(solution)/shard_map/reduce_scatter | solution.py:45
  959.9 509.7 %reduce-scatter.17.cloned.1.call-start = ((), (), s32[]{:S(2)}) async-start(), calls=%async_computation.18 | async-start | bytes 14417920 | tf_op jit(solution)/shard_map/reduce_scatter | solution.py:45
  1006.2 17.4 copy-start.70
  1006.2 17.4 copy-start.71
  1006.2 17.4 copy-start.72
  1006.2 17.4 copy-start.73
  1006.2 17.5 copy-start.47
  1131.4 29.8 copy-start.75
  1142.2 9.4 collective-permute-start.4
  1151.5 8.4 collective-permute-start.5
  1159.9 54.0 %collective-permute-start.6 = (f32[2816]{0:T(1024)S(1)}, f32[2816]{0:T(1024)S(1)}, u32[]{:S(2)}, u32[]{:S(2)}) collective-permute-start(f32[2816]{0:T(1024)S(1)} %multiply_add_fusion.17), channel_id=1, source_target_pairs={{1,0},{2,1},{3,2},{5,4},{6,5},{7,6},{9,8},{10,9},{11,10},{13,12},{... | collective-permute-start | bytes 33800 | tf_op jit(solution)/shard_map/ppermute | solution.py:12
  1191.1 22.7 copy-start.45
  1191.1 22.7 copy-start.49
  1191.1 22.7 copy-start.51
  1248.1 18.5 copy-start.59
  1248.1 18.5 copy-start.61
  1248.1 18.5 copy-start.63
  1248.1 18.5 copy-start.65
  1260.3 6.3 collective-permute-start.7
  1275.7 611.4 %reduce-scatter.25.cloned.1.call-start = ((), (), s32[]{:S(2)}) async-start(), calls=%async_computation.22 | async-start | bytes 31457280 | tf_op jit(solution)/shard_map/reduce_scatter | solution.py:45
  1290.7 1015.3 %reduce-scatter.29.cloned.1.call-start = ((), (), s32[]{:S(2)}) async-start(), calls=%async_computation.24 | async-start | bytes 31457280 | tf_op jit(solution)/shard_map/reduce_scatter | solution.py:45
  1304.6 1419.8 %reduce-scatter.33.cloned.1.call-start = ((), (), s32[]{:S(2)}) async-start(), calls=%async_computation.26 | async-start | bytes 31457280 | tf_op jit(solution)/shard_map/reduce_scatter | solution.py:45
  1319.8 1455.7 %reduce-scatter.39.cloned.1.call-start = ((), (), s32[]{:S(2)}) async-start(), calls=%async_computation.29 | async-start | bytes 3244032
  1324.5 1499.2 %reduce-scatter.23.cloned.1.call-start = ((), (), s32[]{:S(2)}) async-start(), calls=%async_computation.21 | async-start | bytes 3244032 | tf_op jit(solution)/shard_map/reduce_scatter | solution.py:53
  1325.0 1547.7 %reduce-scatter.37.cloned.1.call-start = ((), (), s32[]{:S(2)}) async-start(), calls=%async_computation.28 | async-start | bytes 3244032
  1474.1 1463.7 %reduce-scatter.27.cloned.1.call-start = ((), (), s32[]{:S(2)}) async-start(), calls=%async_computation.23 | async-start | bytes 7077888 | tf_op jit(solution)/shard_map/reduce_scatter | solution.py:53
  1887.2 1115.9 %reduce-scatter.31.cloned.1.call-start = ((), (), s32[]{:S(2)}) async-start(), calls=%async_computation.25 | async-start | bytes 7077888 | tf_op jit(solution)/shard_map/reduce_scatter | solution.py:53
  2305.9 762.1 %reduce-scatter.35.cloned.1.call-start = ((), (), s32[]{:S(2)}) async-start(), calls=%async_computation.27 | async-start | bytes 7077888 | tf_op jit(solution)/shard_map/reduce_scatter | solution.py:53
  2724.4 476.1 %all-reduce.71.cloned.1.call-start = ((), (), s32[]{:S(2)}) async-start(), calls=%async_computation.30 | async-start | bytes 221184 | tf_op jit(solution)/shard_map/psum | solution.py:218
  2744.1 615.2 %all-reduce.73.cloned.1.call-start = ((), (), s32[]{:S(2)}) async-start(), calls=%async_computation.31 | async-start | bytes 11534336 | tf_op jit(solution)/shard_map/psum | solution.py:218
  (97 other events, 686.1 us)
Sparse Core Ops, SparseCore 0:
  10.9 93.9 all-gather.6
  107.7 89.6 all-gather.8
  200.2 89.6 all-gather.10
  292.7 153.0 all-gather.12
  448.5 152.8 all-gather.14
  604.1 152.8 all-gather.16
  832.0 193.1 reduce-scatter.18
  1027.5 196.7 reduce-scatter.20
  1275.9 193.6 reduce-scatter.16
  1471.7 415.4 reduce-scatter.24
  1889.7 416.1 reduce-scatter.28
  2308.1 416.1 reduce-scatter.32
  2728.7 46.7 reduce-scatter.38
  2778.7 44.8 reduce-scatter.22
  2827.8 44.8 reduce-scatter.36
  2876.0 61.6 reduce-scatter.26
  2941.3 61.7 reduce-scatter.30
  3006.4 61.6 reduce-scatter.34
  3076.8 123.6 all-reduce.70
  3206.2 153.0 all-reduce.72
where the time goes:
time: 3400 us; the launch traced here: 3380 us
  waiting for transfers between devices  2420 us (71%)
  local copies, waits for them, and re-layouts  523 us (15%)
  matrix products  236 us (7%)
  other arithmetic  158 us (5%)
    reduce_scatter x6, waiting for transfers between devices, reduce_weight_grad(): lax.psum_scatter(lax.dot_general(left_side, right_side, (((0,), (0,)), ((...  1390 us
    psum x2, waiting for transfers between devices, local(): lax.psum((norm_gain_term, kernel_term, bias_term, recur_w_term, recur_b_t...  289 us
    reduce_scatter x4, waiting for transfers between devices, reduce_weight_grad(): lax.psum_scatter(inner_sum, 'dp', scatter_dimension=1, tiled=True)  234 us
    slice x57, local copies, waits for them, and re-layouts, local(): lax.associative_scan(compose, (next_decay, grad_states), reverse=True, ax...  175 us
    all_gather x1, waiting for transfers between devices, local(): lax.all_gather(mlp_up, ('dp', 'seq'), axis=0, tiled=True)  141 us
    all_gather x1, waiting for transfers between devices, local(): lax.all_gather(mlp_down, ('dp', 'seq'), axis=0, tiled=True)  141 us
    slice x52, local copies, waits for them, and re-layouts, local(): lax.associative_scan(compose, (decay_rate, driven), axis=0)  105 us
    all_gather x1, waiting for transfers between devices, local(): lax.all_gather(in_proj, ('dp', 'seq'), axis=0, tiled=True)  93.3 us
  transfers between devices with their start and end apart: 28, of which 23 were waited for; matrix products, arithmetic and copies ran while one was open for 24% of the time, Pallas kernels for 0%

commit v1 on v0

--- a/solution.py
+++ b/solution.py
@@ -215,20 +215,19 @@
     unused, pull_norm = jax.vjp(scaled_norm, tokens, norm_gain)
     grad_tokens, norm_gain_term = pull_norm(grad_normed)
     input_grad = (grad_tokens + grad_residual).reshape(block_input.shape)
-    summed = lax.psum(
-        (
-            norm_gain_term,
-            kernel_term,
-            bias_term,
-            recur_w_term,
-            recur_b_term,
-            input_w_term,
-            input_b_term,
-            decay_term,
-            mlp_gain_term,
-        ),
-        ("dp", "seq"),
-    )
+    summed = (
+        norm_gain_term,
+        kernel_term,
+        bias_term,
+        recur_w_term,
+        recur_b_term,
+        input_w_term,
+        input_b_term,
+        decay_term,
+        mlp_gain_term,
+    )
+    for over in ("seq", "dp"):
+        summed = lax.psum(summed, over)
     return (
         block_output,
         input_grad,

time: 3400 us -> 3510 us (1.032)
  waiting for transfers between devices: 2420 us -> 2540 us
    psum x2 -> x4, waiting for transfers between devices: 289 us -> 407 us  [local(): summed = lax.psum(summed, over)]
    unnamed x22 -> x24, waiting for transfers between devices: 62.2 us -> 82.4 us
  transfers between devices with their start and end apart: 28 -> 30, of which waited for: 23 -> 25; matrix products, arithmetic and copies ran while one was open for 24% -> 24% of each run, Pallas kernels for 0% -> 0%
where the time goes in v1:
time: 3510 us; the launch traced here: 3490 us
  waiting for transfers between devices  2540 us (72%)
  local copies, waits for them, and re-layouts  523 us (15%)
  matrix products  235 us (7%)
  other arithmetic  158 us (5%)
    reduce_scatter x6, waiting for transfers between devices, reduce_weight_grad(): lax.psum_scatter(lax.dot_general(left_side, right_side, (((0,), (0,)), ((...  1370 us
    psum x4, waiting for transfers between devices, local(): summed = lax.psum(summed, over)  407 us
    reduce_scatter x4, waiting for transfers between devices, reduce_weight_grad(): lax.psum_scatter(inner_sum, 'dp', scatter_dimension=1, tiled=True)  235 us
    slice x57, local copies, waits for them, and re-layouts, local(): lax.associative_scan(compose, (next_decay, grad_states), reverse=True, ax...  175 us
    all_gather x1, waiting for transfers between devices, local(): lax.all_gather(mlp_up, ('dp', 'seq'), axis=0, tiled=True)  141 us
    all_gather x1, waiting for transfers between devices, local(): lax.all_gather(mlp_down, ('dp', 'seq'), axis=0, tiled=True)  141 us
    slice x52, local copies, waits for them, and re-layouts, local(): lax.associative_scan(compose, (decay_rate, driven), axis=0)  105 us
    all_gather x1, waiting for transfers between devices, local(): lax.all_gather(in_proj, ('dp', 'seq'), axis=0, tiled=True)  93.3 us
  transfers between devices with their start and end apart: 30, of which 25 were waited for; matrix products, arithmetic and copies ran while one was open for 24% of the time, Pallas kernels for 0%

profile of v1, /device:TPU:0, one launch (start us, length us, event | category | flops | bytes accessed | tf_op | source)
XLA Modules:
  0.0 3493.8 jit_solution(2600021343039006961)
XLA Ops:
  11.6 93.3 %all-gather.7.cloned.1.call-done = bf16[2048,2816]{1,0:T(8,128)(2,1)} async-done(((bf16[64,2816]{1,0:T(8,128)(2,1)}), bf16[2048,2816]{1,0:T(8,128)(2,1)}) %all-gather.7.cloned.1.call-update) | async-done | bytes 11534352 | tf_op jit(solution)/shard_map/all_gather | solution.py:84
  324.3 9.6 pad.228
  333.9 9.3 pad.229
  345.9 9.4 pad.212
  355.3 9.3 pad.213
  383.9 13.4 multiply_convert_fusion.2
  405.5 40.2 %all-gather.13.cloned.1.call-done = bf16[2048,6144]{1,0:T(8,128)(2,1)} async-done(((bf16[64,6144]{1,0:T(8,128)(2,1)}), bf16[2048,6144]{1,0:T(8,128)(2,1)}) %all-gather.13.cloned.1.call-update) | async-done | bytes 25165840 | tf_op jit(solution)/shard_map/all_gather | solution.py:122
  445.7 14.2 fusion.108
  460.0 141.4 %all-gather.15.cloned.1.call-done = bf16[2048,6144]{1,0:T(8,128)(2,1)} async-done(((bf16[64,6144]{1,0:T(8,128)(2,1)}), bf16[2048,6144]{1,0:T(8,128)(2,1)}) %all-gather.15.cloned.1.call-update) | async-done | bytes 25165840 | tf_op jit(solution)/shard_map/all_gather | solution.py:123
  601.3 14.3 fusion.109
  615.7 141.3 %all-gather.17.cloned.1.call-done = bf16[6144,2048]{1,0:T(8,128)(2,1)} async-done(((bf16[192,2048]{1,0:T(8,128)(2,1)}), bf16[6144,2048]{1,0:T(8,128)(2,1)}) %all-gather.17.cloned.1.call-update) | async-done | bytes 25165840 | tf_op jit(solution)/shard_map/all_gather | solution.py:124
  756.9 22.1 multiply_convert_fusion
  779.1 13.5 fusion.110
  792.6 15.7 multiply_reduce_fusion.5
  811.7 12.8 fusion.45
  853.0 11.9 slice.637
  864.9 11.9 slice.643
  876.7 11.9 slice.695
  900.0 11.9 slice.634
  911.9 11.9 slice.639
  950.4 9.5 convolution_convert_fusion.5
  1068.7 9.5 pad.261
  1091.5 9.4 pad.245
  1100.8 11.9 slice.697
  1119.4 9.4 pad.244
  1131.4 9.6 pad.260
  1168.2 23.0 rev.9
  1191.2 22.7 rev.8
  1248.1 11.9 multiply_reduce_fusion.3
  1276.7 13.7 convolution_convert_fusion.2
  1290.4 13.8 convolution_convert_fusion.1
  1305.5 14.0 convolution_convert_fusion
  1329.1 9.5 fusion.37
  1348.0 121.3 %reduce-scatter.17.cloned.1.call-done = bf16[512,2816]{1,0:T(8,128)(2,1)} async-done(((bf16[2048,2816]{1,0:T(8,128)(2,1)}), bf16[512,2816]{1,0:T(8,128)(2,1)}) %reduce-scatter.17.cloned.1.call-update) | async-done | bytes 2883600 | tf_op jit(solution)/shard_map/reduce_scatter | solution.py:45
  1473.9 413.0 %reduce-scatter.25.cloned.1.call-done = bf16[512,6144]{1,0:T(8,128)(2,1)} async-done(((bf16[2048,6144]{1,0:T(8,128)(2,1)}), bf16[512,6144]{1,0:T(8,128)(2,1)}) %reduce-scatter.25.cloned.1.call-update) | async-done | bytes 6291472 | tf_op jit(solution)/shard_map/reduce_scatter | solution.py:45
  1887.0 418.6 %reduce-scatter.29.cloned.1.call-done = bf16[512,6144]{1,0:T(8,128)(2,1)} async-done(((bf16[2048,6144]{1,0:T(8,128)(2,1)}), bf16[512,6144]{1,0:T(8,128)(2,1)}) %reduce-scatter.29.cloned.1.call-update) | async-done | bytes 6291472 | tf_op jit(solution)/shard_map/reduce_scatter | solution.py:45
  2305.7 418.4 %reduce-scatter.33.cloned.1.call-done = bf16[1536,2048]{1,0:T(8,128)(2,1)} async-done(((bf16[6144,2048]{1,0:T(8,128)(2,1)}), bf16[1536,2048]{1,0:T(8,128)(2,1)}) %reduce-scatter.33.cloned.1.call-update) | async-done | bytes 6291472 | tf_op jit(solution)/shard_map/reduce_scatter | solution.py:45
  2724.1 40.9 %all-reduce.79.cloned.1.call-done = (f32[2048]{0:T(1024)}, f32[4,2816]{1,0:T(4,128)}, f32[2816]{0:T(1024)}, f32[2816]{0:T(1024)}, f32[2816]{0:T(1024)}, /*index=5*/f32[2816]{0:T(1024)}, f32[2048]{0:T(1024)}) async-done(((f32[2048]{0:T(1024)}, f32[4,2816]{1,0:T(4,128)}, f32[2816]{0:T(1024)}, f32[2816]{0:T(1024)}, f32[2816]{0:T(1024)}, /*index=5*/f32[2816]{0:T(1024)}, f32[2048]{0:T(1024)}), (f32[2048]{0:T(1024)}, ...) | async-done | bytes 106512 | tf_op jit(solution)/shard_map/psum | solution.py:230
  2765.1 208.6 %all-reduce.81.cloned.1.call-done = (f32[16,176,176]{2,1,0:T(8,128)}, f32[16,176,176]{2,1,0:T(8,128)}) async-done(((f32[16,176,176]{2,1,0:T(8,128)}, f32[16,176,176]{2,1,0:T(8,128)}), (f32[16,176,176]{2,1,0:T(8,128)}, f32[16,176,176]{2,1,0:T(8,128)})) %all-reduce.81.cloned.1.call-update) | async-done | bytes 3964944 | tf_op jit(solution)/shard_map/psum | solution.py:230
  2973.8 14.6 fusion.35
  2990.3 31.1 reduce-scatter.39.cloned.1.call-done
  3023.7 46.3 %reduce-scatter.23.cloned.1.call-done = bf16[704,256]{1,0:T(8,128)(2,1)} async-done(((bf16[704,2048]{1,0:T(8,128)(2,1)}), bf16[704,256]{1,0:T(8,128)(2,1)}) %reduce-scatter.23.cloned.1.call-update) | async-done | bytes 360464 | tf_op jit(solution)/shard_map/reduce_scatter | solution.py:53
  3071.8 46.8 %reduce-scatter.37.cloned.1.call-done = bf16[352,512]{1,0:T(8,128)(2,1)} async-done(((bf16[2816,512]{1,0:T(8,128)(2,1)}), bf16[352,512]{1,0:T(8,128)(2,1)}) %reduce-scatter.37.cloned.1.call-update) | async-done | bytes 360464
  3120.9 63.1 %reduce-scatter.27.cloned.1.call-done = bf16[512,768]{1,0:T(8,128)(2,1)} async-done(((bf16[512,6144]{1,0:T(8,128)(2,1)}), bf16[512,768]{1,0:T(8,128)(2,1)}) %reduce-scatter.27.cloned.1.call-update) | async-done | bytes 786448 | tf_op jit(solution)/shard_map/reduce_scatter | solution.py:53
  3186.4 62.7 %reduce-scatter.31.cloned.1.call-done = bf16[512,768]{1,0:T(8,128)(2,1)} async-done(((bf16[512,6144]{1,0:T(8,128)(2,1)}), bf16[512,768]{1,0:T(8,128)(2,1)}) %reduce-scatter.31.cloned.1.call-update) | async-done | bytes 786448 | tf_op jit(solution)/shard_map/reduce_scatter | solution.py:53
  3251.6 63.0 %reduce-scatter.35.cloned.1.call-done = bf16[1536,256]{1,0:T(8,128)(2,1)} async-done(((bf16[1536,2048]{1,0:T(8,128)(2,1)}), bf16[1536,256]{1,0:T(8,128)(2,1)}) %reduce-scatter.35.cloned.1.call-update) | async-done | bytes 786448 | tf_op jit(solution)/shard_map/reduce_scatter | solution.py:53
  3317.0 55.0 %all-reduce.75.cloned.1.call-done = (f32[2048]{0:T(1024)}, f32[4,2816]{1,0:T(4,128)}, f32[2816]{0:T(1024)}, f32[2816]{0:T(1024)}, f32[2816]{0:T(1024)}, /*index=5*/f32[2816]{0:T(1024)}, f32[2048]{0:T(1024)}) async-done(((f32[2048]{0:T(1024)}, f32[4,2816]{1,0:T(4,128)}, f32[2816]{0:T(1024)}, f32[2816]{0:T(1024)}, f32[2816]{0:T(1024)}, /*index=5*/f32[2816]{0:T(1024)}, f32[2048]{0:T(1024)}), (f32[2048]{0:T(1024)}, ...) | async-done | bytes 106512 | tf_op jit(solution)/shard_map/psum | solution.py:230
  3372.0 102.9 %all-reduce.77.cloned.1.call-done = (f32[16,176,176]{2,1,0:T(8,128)}, f32[16,176,176]{2,1,0:T(8,128)}) async-done(((f32[16,176,176]{2,1,0:T(8,128)}, f32[16,176,176]{2,1,0:T(8,128)}), (f32[16,176,176]{2,1,0:T(8,128)}, f32[16,176,176]{2,1,0:T(8,128)})) %all-reduce.77.cloned.1.call-update) | async-done | bytes 3964944 | tf_op jit(solution)/shard_map/psum | solution.py:230
  (608 shorter events, 583.8 us)
Async XLA Ops:
  7.2 115.0 %copy-start = (bf16[16,176,176]{2,1,0:T(8,128)(2,1)S(1)}, bf16[16,176,176]{2,1,0:T(8,128)(2,1)}, u32[]{:S(2)}) copy-start(bf16[16,176,176]{2,1,0:T(8,128)(2,1)} %param.23) | copy-start | bytes 2973700
  7.2 97.7 %copy-start.41 = (f32[2048]{0:T(1024)S(1)}, f32[2048]{0:T(1024)}, u32[]{:S(2)}) copy-start(f32[2048]{0:T(1024)} %param.18) | copy-start | bytes 24580
  7.2 97.7 %all-gather.7.cloned.1.call-start = ((), (), s32[]{:S(2)}) async-start(), calls=%async_computation.12 | async-start | bytes 11894784 | tf_op jit(solution)/shard_map/all_gather | solution.py:84
  8.0 374.5 %all-gather.9.cloned.1.call-start = ((), (), s32[]{:S(2)}) async-start(), calls=%async_computation.13 | async-start | bytes 11894784 | tf_op jit(solution)/shard_map/all_gather | solution.py:85
  8.7 388.6 %all-gather.11.cloned.1.call-start = ((), (), s32[]{:S(2)}) async-start(), calls=%async_computation.14 | async-start | bytes 11894784 | tf_op jit(solution)/shard_map/all_gather | solution.py:86
  9.5 436.3 %all-gather.13.cloned.1.call-start = ((), (), s32[]{:S(2)}) async-start(), calls=%async_computation.15 | async-start | bytes 25952256 | tf_op jit(solution)/shard_map/all_gather | solution.py:122
  10.0 591.3 %all-gather.15.cloned.1.call-start = ((), (), s32[]{:S(2)}) async-start(), calls=%async_computation.16 | async-start | bytes 25952256 | tf_op jit(solution)/shard_map/all_gather | solution.py:123
  10.6 746.3 %all-gather.17.cloned.1.call-start = ((), (), s32[]{:S(2)}) async-start(), calls=%async_computation.17 | async-start | bytes 25952256 | tf_op jit(solution)/shard_map/all_gather | solution.py:124
  11.2 1331.5 %reduce-scatter.19.cloned.1.call-start = ((), (), s32[]{:S(2)}) async-start(), calls=%async_computation.19 | async-start | bytes 14417920 | tf_op jit(solution)/shard_map/reduce_scatter | solution.py:45
  11.5 99.7 %copy-start.112 = (f32[256]{0:T(256)}, f32[256]{0:T(256)S(1)}, u32[]{:S(2)}) copy-start(f32[256]{0:T(256)S(1)} %fusion.41) | copy-start | bytes 3076
  11.6 125.2 %copy-start.44 = (f32[2816]{0:T(1024)}, f32[2816]{0:T(1024)S(1)}, u32[]{:S(2)}) copy-start(f32[2816]{0:T(1024)S(1)} %broadcast_multiply_fusion) | copy-start | bytes 33796
  11.6 102.9 %copy-start.97 = (f32[4,2816]{1,0:T(4,128)S(1)}, f32[4,2816]{1,0:T(4,128)}, u32[]{:S(2)}) copy-start(f32[4,2816]{1,0:T(4,128)} %param.21) | copy-start | bytes 135172
  11.6 105.1 %copy-start.108 = (f32[2816]{0:T(1024)S(1)}, f32[2816]{0:T(1024)}, u32[]{:S(2)}) copy-start(f32[2816]{0:T(1024)} %param.22) | copy-start | bytes 33796
  111.3 5.5 collective-permute-start
  366.6 5.7 collective-permute-start.1
  372.3 5.8 collective-permute-start.2
  378.1 5.8 collective-permute-start.3
  405.5 195.9 %copy-start.14 = (bf16[256,2048]{1,0:T(8,128)(2,1)}, bf16[256,2048]{1,0:T(8,128)(2,1)S(1)}, u32[]{:S(2)}) copy-start(bf16[256,2048]{1,0:T(8,128)(2,1)S(1)} %multiply_convert_fusion.3) | copy-start | bytes 3145732
  831.9 515.5 %reduce-scatter.21.cloned.1.call-start = ((), (), s32[]{:S(2)}) async-start(), calls=%async_computation.20 | async-start | bytes 14417920 | tf_op jit(solution)/shard_map/reduce_scatter | solution.py:45
  959.9 509.4 %reduce-scatter.17.cloned.1.call-start = ((), (), s32[]{:S(2)}) async-start(), calls=%async_computation.18 | async-start | bytes 14417920 | tf_op jit(solution)/shard_map/reduce_scatter | solution.py:45
  1006.3 17.3 copy-start.72
  1006.3 17.3 copy-start.73
  1006.3 17.4 copy-start.47
  1131.4 29.9 copy-start.75
  1142.1 9.4 collective-permute-start.4
  1151.6 8.4 collective-permute-start.5
  1160.0 53.9 %collective-permute-start.6 = (f32[2816]{0:T(1024)S(1)}, f32[2816]{0:T(1024)S(1)}, u32[]{:S(2)}, u32[]{:S(2)}) collective-permute-start(f32[2816]{0:T(1024)S(1)} %multiply_add_fusion.17), channel_id=1, source_target_pairs={{1,0},{2,1},{3,2},{5,4},{6,5},{7,6},{9,8},{10,9},{11,10},{13,12},{... | collective-permute-start | bytes 33800 | tf_op jit(solution)/shard_map/ppermute | solution.py:12
  1191.2 22.7 copy-start.45
  1191.2 22.7 copy-start.49
  1191.2 22.7 copy-start.51
  1248.1 18.3 copy-start.59
  1248.1 18.3 copy-start.61
  1248.1 18.3 copy-start.63
  1248.1 18.3 copy-start.65
  1260.0 6.3 collective-permute-start.7
  1275.5 611.5 %reduce-scatter.25.cloned.1.call-start = ((), (), s32[]{:S(2)}) async-start(), calls=%async_computation.22 | async-start | bytes 31457280 | tf_op jit(solution)/shard_map/reduce_scatter | solution.py:45
  1290.4 1015.3 %reduce-scatter.29.cloned.1.call-start = ((), (), s32[]{:S(2)}) async-start(), calls=%async_computation.24 | async-start | bytes 31457280 | tf_op jit(solution)/shard_map/reduce_scatter | solution.py:45
  1304.3 1419.8 %reduce-scatter.33.cloned.1.call-start = ((), (), s32[]{:S(2)}) async-start(), calls=%async_computation.26 | async-start | bytes 31457280 | tf_op jit(solution)/shard_map/reduce_scatter | solution.py:45
  1319.5 1445.5 %all-reduce.79.cloned.1.call-start = ((), (), s32[]{:S(2)}) async-start(), calls=%async_computation.32 | async-start | bytes 221184 | tf_op jit(solution)/shard_map/psum | solution.py:230
  1338.6 1635.1 %all-reduce.81.cloned.1.call-start = ((), (), s32[]{:S(2)}) async-start(), calls=%async_computation.33 | async-start | bytes 11534336 | tf_op jit(solution)/shard_map/psum | solution.py:230
  1342.7 1678.7 %reduce-scatter.39.cloned.1.call-start = ((), (), s32[]{:S(2)}) async-start(), calls=%async_computation.29 | async-start | bytes 3244032
  1347.3 1722.6 %reduce-scatter.23.cloned.1.call-start = ((), (), s32[]{:S(2)}) async-start(), calls=%async_computation.21 | async-start | bytes 3244032 | tf_op jit(solution)/shard_map/reduce_scatter | solution.py:53
  1347.9 1770.7 %reduce-scatter.37.cloned.1.call-start = ((), (), s32[]{:S(2)}) async-start(), calls=%async_computation.28 | async-start | bytes 3244032
  1473.8 1710.2 %reduce-scatter.27.cloned.1.call-start = ((), (), s32[]{:S(2)}) async-start(), calls=%async_computation.23 | async-start | bytes 7077888 | tf_op jit(solution)/shard_map/reduce_scatter | solution.py:53
  1886.9 1362.2 %reduce-scatter.31.cloned.1.call-start = ((), (), s32[]{:S(2)}) async-start(), calls=%async_computation.25 | async-start | bytes 7077888 | tf_op jit(solution)/shard_map/reduce_scatter | solution.py:53
  2305.6 1008.9 %reduce-scatter.35.cloned.1.call-start = ((), (), s32[]{:S(2)}) async-start(), calls=%async_computation.27 | async-start | bytes 7077888 | tf_op jit(solution)/shard_map/reduce_scatter | solution.py:53
  2724.1 647.9 %all-reduce.75.cloned.1.call-start = ((), (), s32[]{:S(2)}) async-start(), calls=%async_computation.30 | async-start | bytes 221184 | tf_op jit(solution)/shard_map/psum | solution.py:230
  2765.1 709.9 %all-reduce.77.cloned.1.call-start = ((), (), s32[]{:S(2)}) async-start(), calls=%async_computation.31 | async-start | bytes 11534336 | tf_op jit(solution)/shard_map/psum | solution.py:230
  (99 other events, 719.8 us)
Sparse Core Ops, SparseCore 0:
  10.9 93.9 all-gather.6
  107.7 89.6 all-gather.8
  200.2 89.6 all-gather.10
  292.7 153.0 all-gather.12
  448.5 152.8 all-gather.14
  604.1 152.8 all-gather.16
  832.1 193.0 reduce-scatter.18
  1027.5 196.7 reduce-scatter.20
  1275.6 193.6 reduce-scatter.16
  1471.5 415.3 reduce-scatter.24
  1889.4 416.1 reduce-scatter.28
  2307.8 416.1 reduce-scatter.32
  2728.3 36.6 all-reduce.78
  2767.3 206.3 all-reduce.80
  2977.5 43.8 reduce-scatter.38
  3025.0 44.8 reduce-scatter.22
  3073.7 44.8 reduce-scatter.36
  3122.3 61.7 reduce-scatter.26
  3187.4 61.7 reduce-scatter.30
  3252.8 61.7 reduce-scatter.34
  3318.5 53.4 all-reduce.74
  3375.7 99.1 all-reduce.76
